TPU v7x, 32 devices: a whole 2x2x4 slice. The times are simulated.
32 devices in a mesh: parts: 2 (over y), tiles: 8 (over z, x), mesh: 2 (over core).
Axes of the slice: x: 2, y: 2, z: 4, core: 2. Of those that a mesh axis runs over, the one named last changes fastest.
Arguments:
- patches: bfloat16 [1024, 128, 128], P(('parts', 'tiles', 'mesh')), parts along dimension 0, may hold values from -6 to 6
- send_index: int32 [32, 32], P(('parts', 'tiles', 'mesh')), parts along dimension 0, may hold values from 0 to 32, as said below
- pair_slots: int32 [32, 2, 16], P(('parts', 'tiles', 'mesh')), parts along dimension 0, may hold values from 0 to 32, as said below
- node_links: int32 [32, 4, 128], P(('parts', 'tiles', 'mesh')), parts along dimension 0, may hold values from 0 to 31
Outputs:
- pair_flow: float32 [2, 512], P(None, ('parts', 'tiles', 'mesh')), parts along dimension 1
- relaxed: float32 [2, 4096], P(None, ('parts', 'tiles', 'mesh')), parts along dimension 1
There are 2 independent parts, one for each index of `parts`. A program takes and returns all parts, laid end to end along the dimension named above; each array names one. Nothing has to cross between parts.
Inputs may be any that keep to these rules, and one draw needn't show every extreme that they name: `send_index`: each patch is sent to at most one owner, as one side of one tile pair; a live pair's two sides come from two different tiles and pair_slots names their received slots, numbered source tile times 4 plus slot; the value 2 * 16 marks an empty send slot. Some device fills all 4 slots to one peer. `pair_slots`: the value 8 * 4 marks a pair slot without a live pair; the number of live pairs differs from owner to owner, and some owner has all 16 slots live.
All inputs are finite; a program needn't handle non-finite values.
Results may differ from a plain program's by a relative error of at most 0.011.
Values may be sent and summed in bfloat16 or wider, within the bound.
No kernel may reach another device: no remote copies, remote signals or barrier semaphores. Data moves between devices by JAX's collectives and lax.ppermute only.
A program may use at most 64 MiB of HBM per device.

v0:
```python
import math
import jax
import jax.numpy as jnp
from jax import lax
from jax.sharding import PartitionSpec as P


def make_tables(side_len):
    ticks = jnp.arange(side_len, dtype=jnp.int32)
    product = ticks[:, None] * ticks[None, :] % side_len
    angle = 2.0 * math.pi / side_len * product.astype(jnp.float32)
    cosine = jnp.cos(angle) / math.sqrt(side_len)
    sine = jnp.sin(angle) / math.sqrt(side_len)
    coord = ticks.astype(jnp.float32)
    gap = coord[:, None] - coord[None, :]
    narrow = jnp.exp(-gap * gap / (2.0 * 0.35 * 0.35)) / (0.35 * math.sqrt(2.0 * math.pi))
    broad = jnp.exp(-gap * gap / 32.0) / (4.0 * math.sqrt(2.0 * math.pi))
    band = narrow - broad
    lag = jnp.where(coord < side_len / 2, coord, coord - side_len)
    return (cosine.astype(jnp.bfloat16), sine.astype(jnp.bfloat16), band.astype(jnp.bfloat16), lag)


def band_pass(stack, band):
    partial_value = jnp.einsum(
        "ij,bjk->bik", band, stack, preferred_element_type=jnp.float32
    ).astype(jnp.bfloat16)
    return jnp.einsum(
        "bij,kj->bik", partial_value, band, preferred_element_type=jnp.float32
    ).astype(jnp.bfloat16)


def prepare(stack, tables):
    cosine, sine, band, lag = tables
    filtered = band_pass(stack, band)
    left = jnp.concatenate([cosine, sine], 0)
    return jnp.einsum("ij,bjk->bik", left, filtered, preferred_element_type=jnp.float32).astype(
        jnp.bfloat16
    )


def finish(halves, tables):
    cosine, sine, band, lag = tables
    side_len = halves.shape[-1]
    count = halves.shape[0] // 2
    right = jnp.concatenate([cosine, sine], 1)
    back_left = jnp.concatenate([cosine, -sine], 1)
    quarter = jnp.einsum("bij,jk->bik", halves, right, preferred_element_type=jnp.float32)
    real_part = quarter[:, :side_len, :side_len] - quarter[:, side_len:, side_len:]
    imag_part = -(quarter[:, :side_len, side_len:] + quarter[:, side_len:, :side_len])
    moving_real, fixed_real = (real_part[:count], real_part[count:])
    moving_imag, fixed_imag = (imag_part[:count], imag_part[count:])
    power_real = moving_real * fixed_real + moving_imag * fixed_imag
    power_imag = moving_imag * fixed_real - moving_real * fixed_imag
    power = jnp.concatenate([power_real, power_imag], 1).astype(jnp.bfloat16)
    mixed = jnp.einsum("bij,jk->bik", power, right, preferred_element_type=jnp.float32)
    first = mixed[:, :side_len, :side_len] - mixed[:, side_len:, side_len:]
    second = mixed[:, :side_len, side_len:] + mixed[:, side_len:, :side_len]
    stacked = jnp.concatenate([first, second], 1).astype(jnp.bfloat16)
    surface = jnp.einsum("ij,bjk->bik", back_left, stacked, preferred_element_type=jnp.float32)
    weight = surface * surface
    denom = jnp.mean(weight, axis=(1, 2)) + 1e-06
    flow_y = jnp.mean(lag[None, :, None] * weight, axis=(1, 2)) / denom
    flow_x = jnp.mean(lag[None, None, :] * weight, axis=(1, 2)) / denom
    return jnp.stack([flow_y, flow_x], 0)


def per_device(patches, send_index, pair_slots, node_links):
    side_len = patches.shape[-1]
    patch_count = patches.shape[0]
    pair_count = pair_slots.shape[-1]
    tile_count = lax.axis_size("tiles")
    tables = make_tables(side_len)
    wanted = send_index[0]
    capacity = wanted.shape[0] // tile_count
    present = wanted < patch_count
    safe_wanted = jnp.minimum(wanted, patch_count - 1)
    picked = patches[safe_wanted]
    picked = jnp.where(present[:, None, None], picked, jnp.zeros_like(picked))
    received = lax.all_to_all(
        picked.reshape((tile_count, capacity) + patches.shape[1:]),
        "tiles",
        split_axis=0,
        concat_axis=0,
        tiled=True,
    )
    slot_total = tile_count * capacity
    received = received.reshape((slot_total,) + received.shape[2:])
    slots = pair_slots[0].reshape(-1)
    valid = slots < slot_total
    chosen = received[jnp.minimum(slots, slot_total - 1)]
    chosen = jnp.where(valid[:, None, None], chosen, jnp.zeros_like(chosen))
    block = min(16, pair_count)
    moving = chosen[:pair_count].reshape((pair_count // block, block) + chosen.shape[1:])
    fixed = chosen[pair_count:].reshape((pair_count // block, block) + chosen.shape[1:])

    def per_block(item):
        moving_part, fixed_part = item
        both = jnp.concatenate([moving_part, fixed_part], 0)
        both = prepare(both, tables)
        return finish(both, tables)

    flows = lax.map(per_block, (moving, fixed))
    pair_flow = jnp.transpose(flows, (1, 0, 2)).reshape(2, pair_count)
    flow_rows = lax.all_gather(pair_flow, "mesh", axis=1, tiled=True)
    linked = flow_rows[:, node_links[0]]
    relaxed = 0.5 * linked[:, 0] + 0.5 * jnp.mean(linked[:, 1:], axis=1)
    return (pair_flow, relaxed)


def solution(mesh):
    placed = (
        P(("parts", "tiles", "mesh"), None, None),
        P(("parts", "tiles", "mesh"), None),
        P(("parts", "tiles", "mesh"), None, None),
        P(("parts", "tiles", "mesh"), None, None),
    )
    return jax.shard_map(
        per_device,
        mesh=mesh,
        in_specs=placed,
        out_specs=(P(None, ("parts", "tiles", "mesh")), P(None, ("parts", "tiles", "mesh"))),
        check_vma=False,
    )
```

profile of v0, /device:TPU:0, one launch (start us, length us, event | category | flops | bytes accessed | tf_op | source)
XLA Modules:
  0.0 55.6 jit_solution(8383764545167968574)
XLA Ops:
  0.6 0.0 copy-start
  0.6 0.7 %fusion.57 = s32[32]{0:T(128)S(1)} fusion(s32[1,32]{1,0:T(1,128)} %param.5), kind=kLoop, calls=%fused_computation.76 | loop fusion | flops 128 | bytes 256 | tf_op jit(solution)/shard_map/select_n | solution.py:77
  1.4 0.7 %compare_reduce_fusion = pred[32]{0:T(512)(128)(4,1)S(1)} fusion(s32[1,32]{1,0:T(1,128)} %param.5), kind=kLoop, calls=%fused_computation.71 | loop fusion | flops 32 | bytes 160 | tf_op jit(solution)/shard_map/lt | solution.py:75
  2.1 0.1 lt.91
  2.2 0.0 copy-done
  2.2 0.8 %gather_fusion = bf16[32,128,128]{2,1,0:T(8,128)(2,1)S(1)} fusion(bf16[32,128,128]{2,1,0:T(8,128)(2,1)S(1)} %copy-done, s32[1024]{0:T(1024)S(1)} %pad_clamp_fusion.2), kind=kCustom, calls=%fused_computation | custom fusion | bytes 2097280 | tf_op jit(solution)/shard_map/gather | solution.py:77
  2.9 0.0 copy-start.2
  2.9 0.0 copy-start.1
  2.9 1.1 %broadcast_select_fusion = bf16[8,4,128,128]{3,2,1,0:T(8,128)(2,1)} fusion(bf16[8,4,128,128]{3,2,1,0:T(8,128)(2,1)S(1)} %bitcast.55, pred[8,4]{1,0:T(8,128)(4,1)S(1)} %lt.91), kind=kLoop, calls=%fused_computation.31 | loop fusion | flops 524288 | bytes 2097184 | tf_op jit(solution)/shard_map/jit(_where)/select_n | solution.py:78
  4.1 7.3 %all-to-all-start = ((bf16[8,4,128,128]{3,2,1,0:T(8,128)(2,1)}), bf16[8,4,128,128]{3,2,1,0:T(8,128)(2,1)S(1)}, u32[]{:S(2)}, u32[]{:S(2)}) async-start(bf16[8,4,128,128]{3,2,1,0:T(8,128)(2,1)} %broadcast_select_fusion), calls=%async_computation | async-start | bytes 2097152 | tf_op jit(solution)/shard_map/all_to_all | solution.py:79
  11.4 0.0 copy-done.2
  11.4 0.1 min.29
  11.5 0.1 lt.89
  11.6 0.0 copy-done.1
  11.6 0.3 fusion.53
  11.9 0.3 multiply_convert_fusion
  12.2 25.0 %all-to-all-done = bf16[8,4,128,128]{3,2,1,0:T(8,128)(2,1)S(1)} async-done(((bf16[8,4,128,128]{3,2,1,0:T(8,128)(2,1)}), bf16[8,4,128,128]{3,2,1,0:T(8,128)(2,1)S(1)}, u32[]{:S(2)}, u32[]{:S(2)}) %all-to-all-start) | async-done | bytes 1048608 | tf_op jit(solution)/shard_map/all_to_all | solution.py:79
  37.1 0.7 %gather_fusion.1 = bf16[32,128,128]{2,1,0:T(8,128)(2,1)S(1)} fusion(bf16[32,128,128]{2,1,0:T(8,128)(2,1)S(1)} %bitcast.54, s32[1024]{0:T(1024)S(1)} %pad_clamp_fusion.1), kind=kCustom, calls=%fused_computation.1 | custom fusion | bytes 2097280 | tf_op jit(solution)/shard_map/gather | solution.py:90
  37.9 1.3 %convolution_convert_fusion = bf16[32,128,128]{2,1,0:T(8,128)(2,1)S(1)} fusion(bf16[32,128,128]{2,1,0:T(8,128)(2,1)S(1)} %gather_fusion.1, pred[32]{0:T(512)(128)(4,1)S(1)} %lt.89, f32[128]{0:T(128)S(1)} %iota_convert_fusion), kind=kOutput, calls=%fused_computation.11 | convolution fusion | flops 270303232 | bytes 2097696 | tf_op jit(solution)/shard_map/while/body/eval_jaxpr/bij,kj->bik/dot_general | solution.py:27
  39.2 5.8 %fusion.1 = f32[32,256,256]{2,1,0:T(8,128)} fusion(bf16[32,128,128]{2,1,0:T(8,128)(2,1)S(1)} %convolution_convert_fusion, bf16[128,128]{1,0:T(8,128)(2,1)S(1)} %get-tuple-element.37, bf16[128,128]{1,0:T(8,128)(2,1)S(1)} %get-tuple-element.38), kind=kOutput, calls=%fused_computation.6 | convolution fusion | flops 806617088 | bytes 9502720 | tf_op jit(solution)/shard_map/while/body/eval_jaxpr/bij,jk->bik/dot_general | solution.py:47
  45.0 4.4 %slice_subtract_fusion = (f32[32,128,128]{2,1,0:T(8,128)S(1)}, f32[32,128,128]{2,1,0:T(8,128)S(1)}) fusion(f32[32,256,256]{2,1,0:T(8,128)} %fusion.1), kind=kLoop, calls=%fused_computation.5 | loop fusion | flops 1572864 | bytes 12582912 | tf_op jit(solution)/shard_map/while/body/eval_jaxpr/sub | solution.py:48
  49.3 0.4 add_convert_fusion
  49.7 0.7 %fusion.9 = f32[16,256,256]{2,1,0:T(8,128)S(1)} fusion(bf16[16,128,128]{2,1,0:T(8,128)(2,1)S(1)} %get-tuple-element.34, bf16[16,128,128]{2,1,0:T(8,128)(2,1)S(1)} %get-tuple-element.33, bf16[128,128]{1,0:T(8,128)(2,1)S(1)} %get-tuple-element.38, bf16[128,128]{1,0:T(8,128)(2,1)S(1)} %get-tuple-element.37), kind=kOutput, calls=%fused_computation.18 | convolution fusion | flops 270663680 | bytes 5308416 | tf_op jit(solution)/shard_map/while/body/eval_jaxpr/bij,jk->bik/dot_general | solution.py:55
  50.4 0.3 fusion.8
  50.7 0.6 %multiply_reduce_fusion.1 = (f32[16]{0:T(128)S(1)}, f32[16]{0:T(128)S(1)}, f32[16]{0:T(128)S(1)}) fusion(f32[128]{0:T(128)S(1)} %compare_select_fusion.3, bf16[128,128]{1,0:T(8,128)(2,1)S(1)} %get-tuple-element.38, bf16[128,128]{1,0:T(8,128)(2,1)S(1)} %fusion.53, bf16[16,128,128]{2,1,0:T(8,128)(2,1)S(1)} %get-tuple-element.32, ...), kind=kOutput, calls=%fused_computation.26 | convolution fusion | flops 138018768 | bytes 1114816 | tf_op jit(solution)/shard_map/while/body/eval_jaxpr/ij,bjk->bik/dot_general | solution.py:59
  51.4 0.6 %pad_maximum_fusion.2 = f32[2,16]{1,0:T(2,128)} fusion(f32[1,16]{1,0:T(1,128)S(1)} %get-tuple-element.36, f32[1,16]{1,0:T(1,128)S(1)} %get-tuple-element.35), kind=kLoop, calls=%fused_computation.75 | loop fusion | flops 32 | bytes 256 | tf_op jit(solution)/shard_map/while/body/eval_jaxpr/stack | solution.py:64
  51.9 1.8 %all-gather = f32[2,16,2]{1,2,0:T(2,128)S(1)} all-gather(f32[1,16,2]{1,2,0:T(2,128)S(1)} %fusion.76), channel_id=1, replica_groups=mesh['parts'=2,'tiles'=8,'mesh'=2] {'mesh'}, dimensions={0}, use_global_device_ids=true | all-gather | bytes 384 | tf_op jit(solution)/shard_map/all_gather | solution.py:104
  53.7 0.1 copy.34
  53.8 1.0 %gather_fusion.2 = f32[512,2]{1,0:T(8,128)S(1)} fusion(f32[2,32]{0,1:T(8,128)S(1)} %bitcast.57, s32[1024]{0:T(1024)S(1)} %pad_clamp_fusion), kind=kCustom, calls=%fused_computation.2 | custom fusion | bytes 10240 | tf_op jit(solution)/shard_map/gather | solution.py:105
  54.9 0.1 copy.28
  55.0 0.6 %fusion.56 = f32[2,128]{1,0:T(2,128)} fusion(f32[2,4,128]{2,0,1:T(2,128)S(1)} %bitcast.59, f32[2,128]{1,0:T(2,128)S(1)} %slice_reduce_fusion), kind=kLoop, calls=%fused_computation.74 | loop fusion | flops 768 | bytes 3072 | tf_op jit(solution)/shard_map/add | solution.py:106
  (12 shorter events, 0.1 us)
Async XLA Ops:
  0.6 1.5 %copy-start = (bf16[32,128,128]{2,1,0:T(8,128)(2,1)S(1)}, bf16[32,128,128]{2,1,0:T(8,128)(2,1)}, u32[]{:S(2)}) copy-start(bf16[32,128,128]{2,1,0:T(8,128)(2,1)} %param.4) | copy-start | bytes 3145732
  2.9 8.4 %copy-start.2 = (s32[1,2,16]{2,1,0:T(2,128)S(1)}, s32[1,2,16]{2,1,0:T(2,128)}, u32[]{:S(2)}) copy-start(s32[1,2,16]{2,1,0:T(2,128)} %param.6) | copy-start | bytes 388
  2.9 8.6 %copy-start.1 = (s32[1,4,128]{2,1,0:T(4,128)S(1)}, s32[1,4,128]{2,1,0:T(4,128)}, u32[]{:S(2)}) copy-start(s32[1,4,128]{2,1,0:T(4,128)} %param.7) | copy-start | bytes 6148
  4.1 33.0 %all-to-all-start = ((bf16[8,4,128,128]{3,2,1,0:T(8,128)(2,1)}), bf16[8,4,128,128]{3,2,1,0:T(8,128)(2,1)S(1)}, u32[]{:S(2)}, u32[]{:S(2)}) async-start(bf16[8,4,128,128]{3,2,1,0:T(8,128)(2,1)} %broadcast_select_fusion), calls=%async_computation | async-start | bytes 2097152 | tf_op jit(solution)/shard_map/all_to_all | solution.py:79
where the time goes:
time: 55.8 us; the launch traced here: 55.6 us
  waiting for transfers between devices  25 us (45%)
  other arithmetic  9.36 us (17%)
  matrix products  8.41 us (15%)
  starting transfers between devices  7.28 us (13%)
  local copies, waits for them, and re-layouts  3 us (5%)
  blocking collectives  1.79 us (3%)
  between operations  0.78 us (1%)
    all_to_all x1, waiting for transfers between devices, per_device(): lax.all_to_all(picked.reshape((tile_count, capacity) + patches.shape[1:])...  25 us
    all_to_all x1, starting transfers between devices, per_device(): lax.all_to_all(picked.reshape((tile_count, capacity) + patches.shape[1:])...  7.28 us
    dot_general x1, matrix products, finish(): jnp.einsum('bij,jk->bik', halves, right, preferred_element_type=jnp.float32)  5.76 us
    sub x1, other arithmetic, finish(): quarter[:, :side_len, :side_len] - quarter[:, side_len:, side_len:]  4.35 us
    all_gather x1, blocking collectives, per_device(): flow_rows = lax.all_gather(pair_flow, 'mesh', axis=1, tiled=True)  1.79 us
    dot_general x1, matrix products, band_pass(): jnp.einsum('bij,kj->bik', partial_value, band, preferred_element_type=jnp...  1.31 us
    gather x2, local copies, waits for them, and re-layouts, per_device(): linked = flow_rows[:, node_links[0]]  1.14 us
    select_n x1, other arithmetic, per_device(): picked = jnp.where(present[:, None, None], picked, jnp.zeros_like(picked))  1.13 us
  transfers between devices with their start and end apart: 1, of which 1 were waited for; matrix products, arithmetic and copies ran while one was open for 1% of the time, Pallas kernels for 0%

commit v1 on v0

--- a/solution.py
+++ b/solution.py
@@ -3,6 +3,22 @@
 import jax.numpy as jnp
 from jax import lax
 from jax.sharding import PartitionSpec as P
+
+
+def swapped_with_each(shard, axis, split, join):
+    ways, here = (lax.axis_size(axis), lax.axis_index(axis))
+    width = shard.shape[split] // ways
+    dims = list(shard.shape)
+    dims[split] = width
+    height = dims[join]
+    dims[join] = height * ways
+    full = jnp.zeros(dims, shard.dtype)
+    for mask in range(ways):
+        part = lax.dynamic_slice_in_dim(shard, (here ^ mask) * width, width, axis=split)
+        if mask:
+            part = lax.ppermute(part, axis, [(d, d ^ mask) for d in range(ways)])
+        full = lax.dynamic_update_slice_in_dim(full, part, (here ^ mask) * height, axis=join)
+    return full
 
 
 def make_tables(side_len):
@@ -76,12 +92,8 @@
     safe_wanted = jnp.minimum(wanted, patch_count - 1)
     picked = patches[safe_wanted]
     picked = jnp.where(present[:, None, None], picked, jnp.zeros_like(picked))
-    received = lax.all_to_all(
-        picked.reshape((tile_count, capacity) + patches.shape[1:]),
-        "tiles",
-        split_axis=0,
-        concat_axis=0,
-        tiled=True,
+    received = swapped_with_each(
+        picked.reshape((tile_count, capacity) + patches.shape[1:]), "tiles", 0, 0
     )
     slot_total = tile_count * capacity
     received = received.reshape((slot_total,) + received.shape[2:])

time: 55.8 us -> 52 us (0.932)
  the two profiles are of different devices: /device:TPU:0 before, /device:TPU:17 now
where the time goes in v1:
time: 52 us; the launch traced here: 51.8 us
  waiting for transfers between devices  18.2 us (35%)
  matrix products  8.41 us (16%)
  other arithmetic  8.36 us (16%)
  starting transfers between devices  7.51 us (14%)
  local copies, waits for them, and re-layouts  5.26 us (10%)
  blocking collectives  3.17 us (6%)
  between operations  0.86 us (2%)
    ppermute x7, waiting for transfers between devices, swapped_with_each(): part = lax.ppermute(part, axis, [(d, d ^ mask) for d in range(ways)])  18.2 us
    ppermute x7, starting transfers between devices, swapped_with_each(): part = lax.ppermute(part, axis, [(d, d ^ mask) for d in range(ways)])  7.51 us
    dot_general x1, matrix products, finish(): jnp.einsum('bij,jk->bik', halves, right, preferred_element_type=jnp.float32)  5.77 us
    sub x1, other arithmetic, finish(): quarter[:, :side_len, :side_len] - quarter[:, side_len:, side_len:]  4.35 us
    all_gather x1, blocking collectives, per_device(): flow_rows = lax.all_gather(pair_flow, 'mesh', axis=1, tiled=True)  3.17 us
    dynamic_update_slice x7, local copies, waits for them, and re-layouts, swapped_with_each(): lax.dynamic_update_slice_in_dim(full, part, (here ^ mask) * height, axis=...  1.93 us
    dot_general x1, matrix products, band_pass(): jnp.einsum('bij,kj->bik', partial_value, band, preferred_element_type=jnp...  1.31 us
    gather x2, local copies, waits for them, and re-layouts, per_device(): linked = flow_rows[:, node_links[0]]  1.14 us
  transfers between devices with their start and end apart: 7, of which 5 were waited for; matrix products, arithmetic and copies ran while one was open for 5% of the time, Pallas kernels for 0%

profile of v1, /device:TPU:17, one launch (start us, length us, event | category | flops | bytes accessed | tf_op | source)
XLA Modules:
  0.0 51.8 jit_solution(15985248138329207789)
XLA Ops:
  0.6 0.0 copy-start
  0.7 0.7 %fusion.57 = s32[32]{0:T(128)S(1)} fusion(s32[1,32]{1,0:T(1,128)} %param.5), kind=kLoop, calls=%fused_computation.91 | loop fusion | flops 128 | bytes 256 | tf_op jit(solution)/shard_map/select_n | solution.py:93
  1.4 0.7 %compare_reduce_fusion = pred[32]{0:T(512)(128)(4,1)S(1)} fusion(s32[1,32]{1,0:T(1,128)} %param.5), kind=kLoop, calls=%fused_computation.86 | loop fusion | flops 32 | bytes 160 | tf_op jit(solution)/shard_map/lt | solution.py:91
  2.1 0.1 lt.123
  2.2 0.0 copy-done
  2.2 0.8 %gather_fusion = bf16[32,128,128]{2,1,0:T(8,128)(2,1)S(1)} fusion(bf16[32,128,128]{2,1,0:T(8,128)(2,1)S(1)} %copy-done, s32[1024]{0:T(1024)S(1)} %pad_clamp_fusion.2), kind=kCustom, calls=%fused_computation | custom fusion | bytes 2097280 | tf_op jit(solution)/shard_map/gather | solution.py:93
  3.0 0.1 broadcast_select_fusion
  3.1 0.0 copy-start.2
  3.1 0.0 copy-start.1
  3.1 0.2 broadcast_in_dim.34
  3.4 0.1 constant_dynamic-slice_fusion
  3.5 1.3 %collective-permute-start = (bf16[1,4,128,128]{3,2,1,0:T(8,128)(2,1)S(1)}, bf16[1,4,128,128]{3,2,1,0:T(8,128)(2,1)}, u32[]{:S(2)}, u32[]{:S(2)}) collective-permute-start(bf16[1,4,128,128]{3,2,1,0:T(8,128)(2,1)S(1)} %get-tuple-element.41), channel_id=1, source_target_pairs={{0,2},{2,0},{4,6},{6,4},{8,10},{10,8},{12,14},{14,12},{1,3},{3,1},... | collective-permute-start | bytes 393224 | tf_op jit(solution)/shard_map/ppermute | solution.py:19
  4.7 1.3 %collective-permute-start.1 = (bf16[1,4,128,128]{3,2,1,0:T(8,128)(2,1)S(1)}, bf16[1,4,128,128]{3,2,1,0:T(8,128)(2,1)}, u32[]{:S(2)}, u32[]{:S(2)}) collective-permute-start(bf16[1,4,128,128]{3,2,1,0:T(8,128)(2,1)S(1)} %get-tuple-element.40), channel_id=1, source_target_pairs={{0,4},{2,6},{4,0},{6,2},{8,12},{10,14},{12,8},{14,10},{1,5},{3,7},... | collective-permute-start | bytes 393224 | tf_op jit(solution)/shard_map/ppermute | solution.py:19
  6.0 0.1 collective-permute-start.2
  6.2 0.0 collective-permute-start.3
  6.2 3.3 %collective-permute-start.4 = (bf16[1,4,128,128]{3,2,1,0:T(8,128)(2,1)S(1)}, bf16[1,4,128,128]{3,2,1,0:T(8,128)(2,1)S(1)}, u32[]{:S(2)}, u32[]{:S(2)}) collective-permute-start(bf16[1,4,128,128]{3,2,1,0:T(8,128)(2,1)S(1)} %get-tuple-element.37), channel_id=1, source_target_pairs={{0,10},{2,8},{4,14},{6,12},{8,2},{10,0},{12,6},{14,4},{1,11},{3,9}... | collective-permute-start | bytes 393224 | tf_op jit(solution)/shard_map/ppermute | solution.py:19
  9.5 0.0 copy-done.2
  9.5 0.3 multiply_convert_fusion
  9.8 0.3 fusion.53
  10.0 0.1 min.29
  10.1 0.0 copy-done.1
  10.2 0.1 lt.121
  10.3 0.0 collective-permute-done
  10.3 0.2 collective-permute-start.5
  10.5 0.9 %constant_dynamic-update-slice_fusion.6 = bf16[8,4,128,128]{3,2,1,0:T(8,128)(2,1)S(1)} fusion(bf16[8,4,128,128]{3,2,1,0:T(8,128)(2,1)S(1)} %get-tuple-element.42, bf16[1,4,128,128]{3,2,1,0:T(8,128)(2,1)} %collective-permute-done, s32[]{:T(128)S(6)} %select_n.105), kind=kLoop, calls=%fused_computation.79 | loop fusion | bytes 262148 | tf_op jit(solution)/shard_map/dynamic_update_slice | solution.py:20
  11.4 0.0 collective-permute-done.1
  11.4 1.3 %collective-permute-start.6 = (bf16[1,4,128,128]{3,2,1,0:T(8,128)(2,1)S(1)}, bf16[1,4,128,128]{3,2,1,0:T(8,128)(2,1)S(1)}, u32[]{:S(2)}, u32[]{:S(2)}) collective-permute-start(bf16[1,4,128,128]{3,2,1,0:T(8,128)(2,1)S(1)} %get-tuple-element.35), channel_id=1, source_target_pairs={{0,14},{2,12},{4,10},{6,8},{8,6},{10,4},{12,2},{14,0},{1,15},{3,13... | collective-permute-start | bytes 393224 | tf_op jit(solution)/shard_map/ppermute | solution.py:19
  12.7 0.9 %constant_dynamic-update-slice_fusion.5 = bf16[8,4,128,128]{3,2,1,0:T(8,128)(2,1)S(1)} fusion(bf16[8,4,128,128]{3,2,1,0:T(8,128)(2,1)S(1)} %constant_dynamic-update-slice_fusion.6, bf16[1,4,128,128]{3,2,1,0:T(8,128)(2,1)} %collective-permute-done.1, s32[]{:T(128)S(6)} %select_n.106), kind=kLoop, calls=%fused_computation.77 | loop fusion | bytes 262148 | tf_op jit(solution)/shard_map/dynamic_update_slice | solution.py:20
  13.6 0.1 collective-permute-done.2
  13.7 0.4 collective-permute-done.3
  14.2 2.8 %collective-permute-done.4 = bf16[1,4,128,128]{3,2,1,0:T(8,128)(2,1)S(1)} collective-permute-done((bf16[1,4,128,128]{3,2,1,0:T(8,128)(2,1)S(1)}, bf16[1,4,128,128]{3,2,1,0:T(8,128)(2,1)S(1)}, u32[]{:S(2)}, u32[]{:S(2)}) %collective-permute-start.4) | collective-permute-done | bytes 131104 | tf_op jit(solution)/shard_map/ppermute | solution.py:19
  17.0 10.6 %collective-permute-done.5 = bf16[1,4,128,128]{3,2,1,0:T(8,128)(2,1)S(1)} collective-permute-done((bf16[1,4,128,128]{3,2,1,0:T(8,128)(2,1)S(1)}, bf16[1,4,128,128]{3,2,1,0:T(8,128)(2,1)S(1)}, u32[]{:S(2)}, u32[]{:S(2)}) %collective-permute-start.5) | collective-permute-done | bytes 131104 | tf_op jit(solution)/shard_map/ppermute | solution.py:19
  27.6 4.4 %collective-permute-done.6 = bf16[1,4,128,128]{3,2,1,0:T(8,128)(2,1)S(1)} collective-permute-done((bf16[1,4,128,128]{3,2,1,0:T(8,128)(2,1)S(1)}, bf16[1,4,128,128]{3,2,1,0:T(8,128)(2,1)S(1)}, u32[]{:S(2)}, u32[]{:S(2)}) %collective-permute-start.6) | collective-permute-done | bytes 131104 | tf_op jit(solution)/shard_map/ppermute | solution.py:19
  32.0 0.7 %gather_fusion.1 = bf16[32,128,128]{2,1,0:T(8,128)(2,1)S(1)} fusion(bf16[32,128,128]{2,1,0:T(8,128)(2,1)S(1)} %bitcast.54, s32[1024]{0:T(1024)S(1)} %pad_clamp_fusion.1), kind=kCustom, calls=%fused_computation.1 | custom fusion | bytes 2097280 | tf_op jit(solution)/shard_map/gather | solution.py:102
  32.7 1.3 %convolution_convert_fusion = bf16[32,128,128]{2,1,0:T(8,128)(2,1)S(1)} fusion(bf16[32,128,128]{2,1,0:T(8,128)(2,1)S(1)} %gather_fusion.1, pred[32]{0:T(512)(128)(4,1)S(1)} %lt.121, f32[128]{0:T(128)S(1)} %iota_convert_fusion), kind=kOutput, calls=%fused_computation.11 | convolution fusion | flops 270303232 | bytes 2097696 | tf_op jit(solution)/shard_map/while/body/eval_jaxpr/bij,kj->bik/dot_general | solution.py:43
  34.1 5.8 %fusion.1 = f32[32,256,256]{2,1,0:T(8,128)} fusion(bf16[32,128,128]{2,1,0:T(8,128)(2,1)S(1)} %convolution_convert_fusion, bf16[128,128]{1,0:T(8,128)(2,1)S(1)} %get-tuple-element.45, bf16[128,128]{1,0:T(8,128)(2,1)S(1)} %get-tuple-element.46), kind=kOutput, calls=%fused_computation.6 | convolution fusion | flops 806617088 | bytes 9502720 | tf_op jit(solution)/shard_map/while/body/eval_jaxpr/bij,jk->bik/dot_general | solution.py:63
  39.8 4.4 %slice_subtract_fusion = (f32[32,128,128]{2,1,0:T(8,128)S(1)}, f32[32,128,128]{2,1,0:T(8,128)S(1)}) fusion(f32[32,256,256]{2,1,0:T(8,128)} %fusion.1), kind=kLoop, calls=%fused_computation.5 | loop fusion | flops 1572864 | bytes 12582912 | tf_op jit(solution)/shard_map/while/body/eval_jaxpr/sub | solution.py:64
  44.2 0.4 add_convert_fusion
  44.6 0.7 %fusion.9 = f32[16,256,256]{2,1,0:T(8,128)S(1)} fusion(bf16[16,128,128]{2,1,0:T(8,128)(2,1)S(1)} %get-tuple-element.34, bf16[16,128,128]{2,1,0:T(8,128)(2,1)S(1)} %get-tuple-element.33, bf16[128,128]{1,0:T(8,128)(2,1)S(1)} %get-tuple-element.46, bf16[128,128]{1,0:T(8,128)(2,1)S(1)} %get-tuple-element.45), kind=kOutput, calls=%fused_computation.18 | convolution fusion | flops 270663680 | bytes 5308416 | tf_op jit(solution)/shard_map/while/body/eval_jaxpr/bij,jk->bik/dot_general | solution.py:71
  45.3 0.3 fusion.8
  45.6 0.6 %multiply_reduce_fusion.1 = (f32[16]{0:T(128)S(1)}, f32[16]{0:T(128)S(1)}, f32[16]{0:T(128)S(1)}) fusion(f32[128]{0:T(128)S(1)} %compare_select_fusion.3, bf16[128,128]{1,0:T(8,128)(2,1)S(1)} %get-tuple-element.46, bf16[128,128]{1,0:T(8,128)(2,1)S(1)} %fusion.53, bf16[16,128,128]{2,1,0:T(8,128)(2,1)S(1)} %get-tuple-element.32, ...), kind=kOutput, calls=%fused_computation.26 | convolution fusion | flops 138018768 | bytes 1114816 | tf_op jit(solution)/shard_map/while/body/eval_jaxpr/ij,bjk->bik/dot_general | solution.py:75
  46.2 0.6 %pad_maximum_fusion.2 = f32[2,16]{1,0:T(2,128)} fusion(f32[1,16]{1,0:T(1,128)S(1)} %get-tuple-element.44, f32[1,16]{1,0:T(1,128)S(1)} %get-tuple-element.43), kind=kLoop, calls=%fused_computation.90 | loop fusion | flops 32 | bytes 256 | tf_op jit(solution)/shard_map/while/body/eval_jaxpr/stack | solution.py:80
  46.8 3.2 %all-gather = f32[2,16,2]{1,2,0:T(2,128)S(1)} all-gather(f32[1,16,2]{1,2,0:T(2,128)S(1)} %fusion.76), channel_id=1, replica_groups=mesh['parts'=2,'tiles'=8,'mesh'=2] {'mesh'}, dimensions={0}, use_global_device_ids=true | all-gather | bytes 384 | tf_op jit(solution)/shard_map/all_gather | solution.py:116
  50.0 0.1 copy.34
  50.1 1.0 %gather_fusion.2 = f32[512,2]{1,0:T(8,128)S(1)} fusion(f32[2,32]{0,1:T(8,128)S(1)} %bitcast.57, s32[1024]{0:T(1024)S(1)} %pad_clamp_fusion), kind=kCustom, calls=%fused_computation.2 | custom fusion | bytes 10240 | tf_op jit(solution)/shard_map/gather | solution.py:117
  51.1 0.1 copy.28
  51.2 0.6 %fusion.56 = f32[2,128]{1,0:T(2,128)} fusion(f32[2,4,128]{2,0,1:T(2,128)S(1)} %bitcast.59, f32[2,128]{1,0:T(2,128)S(1)} %slice_reduce_fusion), kind=kLoop, calls=%fused_computation.89 | loop fusion | flops 768 | bytes 3072 | tf_op jit(solution)/shard_map/add | solution.py:118
  (17 shorter events, 0.2 us)
Async XLA Ops:
  0.6 1.6 %copy-start = (bf16[32,128,128]{2,1,0:T(8,128)(2,1)S(1)}, bf16[32,128,128]{2,1,0:T(8,128)(2,1)}, u32[]{:S(2)}) copy-start(bf16[32,128,128]{2,1,0:T(8,128)(2,1)} %param.4) | copy-start | bytes 3145732
  3.1 6.4 %copy-start.2 = (s32[1,2,16]{2,1,0:T(2,128)S(1)}, s32[1,2,16]{2,1,0:T(2,128)}, u32[]{:S(2)}) copy-start(s32[1,2,16]{2,1,0:T(2,128)} %param.6) | copy-start | bytes 388
  3.1 7.0 %copy-start.1 = (s32[1,4,128]{2,1,0:T(4,128)S(1)}, s32[1,4,128]{2,1,0:T(4,128)}, u32[]{:S(2)}) copy-start(s32[1,4,128]{2,1,0:T(4,128)} %param.7) | copy-start | bytes 6148
  3.5 6.8 %collective-permute-start = (bf16[1,4,128,128]{3,2,1,0:T(8,128)(2,1)S(1)}, bf16[1,4,128,128]{3,2,1,0:T(8,128)(2,1)}, u32[]{:S(2)}, u32[]{:S(2)}) collective-permute-start(bf16[1,4,128,128]{3,2,1,0:T(8,128)(2,1)S(1)} %get-tuple-element.41), channel_id=1, source_target_pairs={{0,2},{2,0},{4,6},{6,4},{8,10},{10,8},{12,14},{14,12},{1,3},{3,1},... | collective-permute-start | bytes 393224 | tf_op jit(solution)/shard_map/ppermute | solution.py:19
  4.7 6.6 %collective-permute-start.1 = (bf16[1,4,128,128]{3,2,1,0:T(8,128)(2,1)S(1)}, bf16[1,4,128,128]{3,2,1,0:T(8,128)(2,1)}, u32[]{:S(2)}, u32[]{:S(2)}) collective-permute-start(bf16[1,4,128,128]{3,2,1,0:T(8,128)(2,1)S(1)} %get-tuple-element.40), channel_id=1, source_target_pairs={{0,4},{2,6},{4,0},{6,2},{8,12},{10,14},{12,8},{14,10},{1,5},{3,7},... | collective-permute-start | bytes 393224 | tf_op jit(solution)/shard_map/ppermute | solution.py:19
  6.0 7.7 %collective-permute-start.2 = (bf16[1,4,128,128]{3,2,1,0:T(8,128)(2,1)S(1)}, bf16[1,4,128,128]{3,2,1,0:T(8,128)(2,1)S(1)}, u32[]{:S(2)}, u32[]{:S(2)}) collective-permute-start(bf16[1,4,128,128]{3,2,1,0:T(8,128)(2,1)S(1)} %get-tuple-element.39), channel_id=1, source_target_pairs={{0,6},{2,4},{4,2},{6,0},{8,14},{10,12},{12,10},{14,8},{1,7},{3,5},... | collective-permute-start | bytes 393224 | tf_op jit(solution)/shard_map/ppermute | solution.py:19
  6.2 8.0 %collective-permute-start.3 = (bf16[1,4,128,128]{3,2,1,0:T(8,128)(2,1)S(1)}, bf16[1,4,128,128]{3,2,1,0:T(8,128)(2,1)S(1)}, u32[]{:S(2)}, u32[]{:S(2)}) collective-permute-start(bf16[1,4,128,128]{3,2,1,0:T(8,128)(2,1)S(1)} %get-tuple-element.38), channel_id=1, source_target_pairs={{0,8},{2,10},{4,12},{6,14},{8,0},{10,2},{12,4},{14,6},{1,9},{3,11}... | collective-permute-start | bytes 393224 | tf_op jit(solution)/shard_map/ppermute | solution.py:19
  6.2 10.8 %collective-permute-start.4 = (bf16[1,4,128,128]{3,2,1,0:T(8,128)(2,1)S(1)}, bf16[1,4,128,128]{3,2,1,0:T(8,128)(2,1)S(1)}, u32[]{:S(2)}, u32[]{:S(2)}) collective-permute-start(bf16[1,4,128,128]{3,2,1,0:T(8,128)(2,1)S(1)} %get-tuple-element.37), channel_id=1, source_target_pairs={{0,10},{2,8},{4,14},{6,12},{8,2},{10,0},{12,6},{14,4},{1,11},{3,9}... | collective-permute-start | bytes 393224 | tf_op jit(solution)/shard_map/ppermute | solution.py:19
  10.3 17.3 %collective-permute-start.5 = (bf16[1,4,128,128]{3,2,1,0:T(8,128)(2,1)S(1)}, bf16[1,4,128,128]{3,2,1,0:T(8,128)(2,1)S(1)}, u32[]{:S(2)}, u32[]{:S(2)}) collective-permute-start(bf16[1,4,128,128]{3,2,1,0:T(8,128)(2,1)S(1)} %get-tuple-element.36), channel_id=1, source_target_pairs={{0,12},{2,14},{4,8},{6,10},{8,4},{10,6},{12,0},{14,2},{1,13},{3,15... | collective-permute-start | bytes 393224 | tf_op jit(solution)/shard_map/ppermute | solution.py:19
  11.4 20.6 %collective-permute-start.6 = (bf16[1,4,128,128]{3,2,1,0:T(8,128)(2,1)S(1)}, bf16[1,4,128,128]{3,2,1,0:T(8,128)(2,1)S(1)}, u32[]{:S(2)}, u32[]{:S(2)}) collective-permute-start(bf16[1,4,128,128]{3,2,1,0:T(8,128)(2,1)S(1)} %get-tuple-element.35), channel_id=1, source_target_pairs={{0,14},{2,12},{4,10},{6,8},{8,6},{10,4},{12,2},{14,0},{1,15},{3,13... | collective-permute-start | bytes 393224 | tf_op jit(solution)/shard_map/ppermute | solution.py:19
